TPU v7x, 128 devices: a whole 4x4x4 slice. The times are simulated.
128 devices in a mesh: gy: 8 (over z_lo, x), gz: 16 (over y, z_hi, core).
Axes of the slice: x: 4, y: 4, z: 4 (z_hi: 2, z_lo: 2; z = z_hi * 2 + z_lo), core: 2. Of those that a mesh axis runs over, the one named last changes fastest.
Arguments:
- density: float32 [1024, 128, 256], P('gy', 'gz'), may hold values from 0.5 to 2
- momentum: float32 [3, 1024, 128, 256], P(None, 'gy', 'gz'), may hold values from -3 to 3
- energy: float32 [1024, 128, 256], P('gy', 'gz'), may hold values from 2 to 4
- wall_operator: float32 [1024, 1024], replicated, may hold values from -0.1875 to 0.1875
- span_operator: float32 [128, 128], replicated, may hold values from -0.5 to 0.5
- damping: float32 [1024], replicated, may hold values from 0.1 to 1
Outputs:
- new_density: float32 [1024, 128, 256], P('gy', 'gz')
- new_momentum: float32 [3, 1024, 128, 256], P(None, 'gy', 'gz')
- new_energy: float32 [1024, 128, 256], P('gy', 'gz')
All inputs are finite; a program needn't handle non-finite values.
Results may differ from a plain program's by a relative error of at most 0.00009.
Values sent between devices are 32-bit elements; how exact they have to be, the bound alone decides.
A program may use at most 256 MiB of HBM per device.

v0:
```python
import jax
import jax.numpy as jnp
from jax import lax
from jax.sharding import PartitionSpec as P

gamma_less = 0.4
time_step = 0.1


def with_halo(cells, sides, width, closed):
    for axis, dim in sides:
        count = lax.axis_size(axis)
        ends = count if closed else count - 1
        head = lax.slice_in_dim(cells, 0, width, axis=dim)
        tail = lax.slice_in_dim(cells, cells.shape[dim] - width, cells.shape[dim], axis=dim)
        cells = jnp.concatenate(
            [
                lax.ppermute(tail, axis, [(i, (i + 1) % count) for i in range(ends)]),
                cells,
                lax.ppermute(head, axis, [((i + 1) % count, i) for i in range(ends)]),
            ],
            axis=dim,
        )
    return cells


def flux_along(conserved, direction):
    velocity = conserved[1 + direction] / conserved[0]
    kinetic = (
        0.5
        * (conserved[1] * conserved[1] + conserved[2] * conserved[2] + conserved[3] * conserved[3])
        / conserved[0]
    )
    pressure = gamma_less * (conserved[4] - kinetic)
    components = [conserved[1 + direction]]
    for column in range(3):
        product = conserved[1 + column] * velocity
        if column == direction:
            product = product + pressure
        components.append(product)
    components.append((conserved[4] + pressure) * velocity)
    return jnp.stack(components)


def x_derivative(flux_field):
    widths = [(0, 0)] * (flux_field.ndim - 1) + [(2, 2)]
    padded = jnp.pad(flux_field, widths, mode="edge")
    return (
        8.0 * (padded[..., 3:-1] - padded[..., 1:-3]) - (padded[..., 4:] - padded[..., :-4])
    ) / 12.0


def fourth_difference(padded, along_axis, length_out):

    def shifted(offset):
        return lax.slice_in_dim(padded, offset, offset + length_out, axis=along_axis)

    return shifted(0) - 4.0 * shifted(1) + 6.0 * shifted(2) - 4.0 * shifted(3) + shifted(4)


def local(density, momentum, energy, wall_operator, span_operator, damping):
    conserved = jnp.concatenate([density[None], momentum, energy[None]], axis=0)
    rows_here = conserved.shape[1]
    planes_here = conserved.shape[2]
    first_row = lax.axis_index("gy") * rows_here
    local_damping = lax.dynamic_slice_in_dim(damping, first_row, rows_here)
    along_x = x_derivative(flux_along(conserved, 0))
    upward = flux_along(conserved, 1)
    sideways = flux_along(conserved, 2)
    derivative = jnp.einsum(
        "ij,fjzx->fizx",
        wall_operator,
        lax.all_to_all(upward, "gy", split_axis=3, concat_axis=1, tiled=True),
        precision=lax.Precision.HIGHEST,
    )
    deriv_y = lax.all_to_all(derivative, "gy", split_axis=1, concat_axis=3, tiled=True)
    derivative = jnp.einsum(
        "ij,fyjx->fyix",
        span_operator,
        lax.all_to_all(sideways, "gz", split_axis=3, concat_axis=2, tiled=True),
        precision=lax.Precision.HIGHEST,
    )
    deriv_z = lax.all_to_all(derivative, "gz", split_axis=2, concat_axis=3, tiled=True)
    near_y = with_halo(conserved, (("gy", 1),), 2, False)
    near_z = with_halo(conserved, (("gz", 2),), 2, True)
    smoothing = fourth_difference(near_y, 1, rows_here) + fourth_difference(near_z, 2, planes_here)
    tendency = -along_x - deriv_y - deriv_z - local_damping[None, :, None, None] * smoothing
    advanced = conserved + time_step * tendency
    return (advanced[0], advanced[1:4], advanced[4])


def solution(mesh):
    in_specs = (P("gy", "gz", None), P(None, "gy", "gz", None), P("gy", "gz", None), P(), P(), P())
    out_specs = (P("gy", "gz", None), P(None, "gy", "gz", None), P("gy", "gz", None))
    return jax.shard_map(local, mesh=mesh, in_specs=in_specs, out_specs=out_specs, check_vma=False)
```

profile of v0, /device:TPU:87, one launch (start us, length us, event | category | flops | bytes accessed | tf_op | source)
XLA Modules:
  0.0 498.6 jit_solution(11741611885511762760)
XLA Ops:
  0.6 0.0 copy-start
  0.6 2.7 copy.70
  3.3 2.6 copy.71
  5.9 2.6 copy.72
  8.5 0.1 slice_dynamic-update-slice_fusion
  8.6 0.0 copy-start.2
  8.6 0.0 copy-start.5
  8.6 1.5 bitcast_dynamic-update-slice_fusion.3
  10.2 0.2 slice_dynamic-update-slice_fusion.2
  10.4 0.1 copy-done.5
  10.5 0.4 bitcast_dynamic-update-slice_fusion.1
  10.9 0.3 bitcast_dynamic-update-slice_fusion.11
  11.2 0.1 bitcast_dynamic-update-slice_fusion.10
  11.3 0.2 bitcast_dynamic-update-slice_fusion.9
  11.5 0.1 bitcast_dynamic-update-slice_fusion.5
  11.6 0.3 bitcast_dynamic-update-slice_fusion
  11.9 2.3 copy-done.7
  14.2 2.3 copy-done.8
  16.5 2.7 copy.81
  19.2 5.3 %all-to-all-start = ((f32[5,128,8,256]{1,2,0,3:T(8,128)}), f32[5,128,8,256]{1,2,0,3:T(8,128)}, u32[]{:S(2)}, u32[]{:S(2)}) async-start(f32[5,128,8,256]{1,2,0,3:T(8,128)} %copy.81), calls=%async_computation | async-start | bytes 10485760 | tf_op jit(solution)/shard_map/all_to_all | solution.py:73
  24.5 5.1 %copy.89 = f32[5,128,8,256]{1,2,0,3:T(8,128)} copy(f32[5,128,8,256]{1,2,3,0:T(8,128)} %copy-done.8) | data formatting | bytes 10485760 | tf_op jit(solution)/shard_map/stack | solution.py:42
  29.7 71.1 %all-to-all-done = f32[5,128,8,256]{1,2,0,3:T(8,128)} async-done(((f32[5,128,8,256]{1,2,0,3:T(8,128)}), f32[5,128,8,256]{1,2,0,3:T(8,128)}, u32[]{:S(2)}, u32[]{:S(2)}) %all-to-all-start) | async-done | bytes 5242912 | tf_op jit(solution)/shard_map/all_to_all | solution.py:73
  100.8 8.7 %all-to-all-start.2 = ((f32[5,128,8,256]{1,2,0,3:T(8,128)}), f32[5,128,8,256]{1,2,0,3:T(8,128)}, u32[]{:S(2)}, u32[]{:S(2)}) async-start(f32[5,128,8,256]{1,2,0,3:T(8,128)} %copy.89), calls=%async_computation.2 | async-start | bytes 10485760 | tf_op jit(solution)/shard_map/all_to_all | solution.py:80
  109.5 7.9 %copy.83 = f32[5,8,128,8,32]{2,1,4,3,0:T(8,128)} copy(f32[5,8,128,8,32]{2,3,0,4,1:T(8,128)} %bitcast.17) | data formatting | bytes 10485760 | tf_op jit(solution)/shard_map/all_to_all | solution.py:73
  117.4 6.8 %all_to_all.55 = f32[5,1024,8,32]{1,3,2,0:T(8,128)} reshape(f32[5,8,128,8,32]{2,1,4,3,0:T(8,128)} %copy.83) | data formatting | bytes 10485760 | tf_op jit(solution)/shard_map/all_to_all | solution.py:73
  124.2 22.0 %fusion.25 = f32[5,1024,8,32]{1,3,2,0:T(8,128)} fusion(f32[5,1024,8,32]{1,3,2,0:T(8,128)} %all_to_all.55, f32[1024,1024]{1,0:T(8,128)} %param.9), kind=kOutput, calls=%fused_computation.42 | convolution fusion | flops 16106127360 | bytes 14680064 | tf_op jit(solution)/shard_map/ij,fjzx->fizx/dot_general | solution.py:70
  146.1 13.3 %copy.84 = f32[5,1024,8,32]{3,2,0,1:T(8,128)} copy(f32[5,1024,8,32]{1,3,2,0:T(8,128)} %fusion.25) | data formatting | bytes 10485760 | tf_op jit(solution)/shard_map/ij,fjzx->fizx/transpose | solution.py:70
  159.4 14.8 %reshape.21 = f32[8,1,163840]{2,1,0:T(1,128)} reshape(f32[1024,5,8,32]{3,2,1,0:T(8,128)} %bitcast.138) | data formatting | bytes 10485760
  174.2 15.9 %all-to-all-done.2 = f32[5,128,8,256]{1,2,0,3:T(8,128)} async-done(((f32[5,128,8,256]{1,2,0,3:T(8,128)}), f32[5,128,8,256]{1,2,0,3:T(8,128)}, u32[]{:S(2)}, u32[]{:S(2)}) %all-to-all-start.2) | async-done | bytes 5242912 | tf_op jit(solution)/shard_map/all_to_all | solution.py:80
  190.1 16.9 %all-to-all-start.1 = ((f32[8,1,163840]{2,1,0:T(1,128)}), f32[8,1,163840]{2,1,0:T(1,128)}, u32[]{:S(2)}, u32[]{:S(2)}) async-start(f32[8,1,163840]{2,1,0:T(1,128)} %reshape.21), calls=%async_computation.1 | async-start | bytes 10485760 | tf_op jit(solution)/shard_map/all_to_all | solution.py:76
  207.0 3.7 copy.91
  210.7 11.4 %fusion.28 = f32[5,128,128,16]{2,1,3,0:T(8,128)} fusion(f32[5,128,128,16]{1,3,2,0:T(8,128)S(1)} %bitcast.150, f32[128,128]{1,0:T(8,128)S(1)} %copy-done), kind=kOutput, calls=%fused_computation.43 | convolution fusion | flops 2013265920 | bytes 10551296 | tf_op jit(solution)/shard_map/ij,fyjx->fyix/dot_general | solution.py:77
  222.1 6.1 %copy.93 = f32[5,128,128,16]{1,3,0,2:T(8,128)} copy(f32[5,128,128,16]{2,1,3,0:T(8,128)} %fusion.28) | data formatting | bytes 10485760 | tf_op jit(solution)/shard_map/ij,fyjx->fyix/transpose | solution.py:77
  228.2 56.2 %all-to-all-done.1 = f32[8,1,163840]{2,1,0:T(1,128)} async-done(((f32[8,1,163840]{2,1,0:T(1,128)}), f32[8,1,163840]{2,1,0:T(1,128)}, u32[]{:S(2)}, u32[]{:S(2)}) %all-to-all-start.1) | async-done | bytes 5242912 | tf_op jit(solution)/shard_map/all_to_all | solution.py:76
  284.4 8.1 %all-to-all-start.3 = ((f32[5,128,128,16]{1,3,0,2:T(8,128)}), f32[5,128,128,16]{1,3,0,2:T(8,128)}, u32[]{:S(2)}, u32[]{:S(2)}) async-start(f32[5,128,128,16]{1,3,0,2:T(8,128)} %copy.93), calls=%async_computation.3 | async-start | bytes 10485760 | tf_op jit(solution)/shard_map/all_to_all | solution.py:83
  292.6 1.9 pad_maximum_fusion.4
  294.5 2.3 fusion.43
  296.8 1.2 collective-permute-start.2
  297.9 0.0 collective-permute-start.3
  298.0 5.6 %fusion.42 = (f32[5,2,8,256]{1,2,3,0:T(8,128)}, f32[5,2,8,256]{1,2,3,0:T(8,128)}) fusion(f32[5,128,8,256]{1,2,3,0:T(8,128)S(1)} %pad_maximum_fusion.4), kind=kLoop, calls=%fused_computation.88 | loop fusion | bytes 327680 | tf_op jit(solution)/shard_map/slice | solution.py:15
  303.5 3.3 copy.99
  306.8 1.9 collective-permute-start.1
  308.7 3.3 copy.97
  312.1 5.5 %collective-permute-start = (f32[5,2,8,256]{3,2,1,0:T(8,128)S(1)}, f32[5,2,8,256]{3,2,1,0:T(8,128)}, u32[]{:S(2)}, u32[]{:S(2)}) collective-permute-start(f32[5,2,8,256]{3,2,1,0:T(8,128)S(1)} %copy.97), channel_id=1, source_target_pairs={{0,16},{16,32},{32,48},{48,64},{64,80},{80,96},{96,112},{1,17},{17... | collective-permute-start | bytes 245768 | tf_op jit(solution)/shard_map/ppermute | solution.py:18
  317.5 0.8 slice_bitcast_fusion.3
  318.3 0.8 dynamic_slice.3
  319.0 0.0 collective-permute-done
  319.1 3.9 copy.98
  323.0 3.1 copy.100
  326.1 14.6 %maximum_maximum_fusion = (f32[5,130,8,256]{1,2,3,0:T(8,128)}, f32[5,130,8,256]{1,2,3,0:T(8,128)}) fusion(f32[1,128,8,256]{1,2,3,0:T(8,128)} %bitcast.145, f32[3,128,8,256]{1,2,3,0:T(8,128)S(1)} %copy.72, f32[1,128,8,256]{1,2,3,0:T(8,128)} %bitcast.141, f32[5,2,8,256]{1,2,3,0:T(8,128)} %copy.98, f32[5,2,8,256]{1,2,3,0:T(8,128)} %copy.100), kind=kLoop, calls=%fused_computation | loop fusion | flops 7987200 | bytes 16056320 | tf_op jit(solution)/shard_map/concatenate | solution.py:16
  340.7 23.0 %collective-permute-done.2 = f32[5,128,2,256]{1,2,3,0:T(2,128)} collective-permute-done((f32[5,128,2,256]{1,2,3,0:T(2,128)}, f32[5,128,2,256]{1,2,3,0:T(2,128)}, u32[]{:S(2)}, u32[]{:S(2)}) %collective-permute-start.2) | collective-permute-done | bytes 1310752 | tf_op jit(solution)/shard_map/ppermute | solution.py:18
  363.7 24.3 %collective-permute-done.3 = f32[5,128,2,256]{1,2,3,0:T(2,128)} collective-permute-done((f32[5,128,2,256]{1,2,3,0:T(2,128)}, f32[5,128,2,256]{1,2,3,0:T(2,128)}, u32[]{:S(2)}, u32[]{:S(2)}) %collective-permute-start.3) | collective-permute-done | bytes 1310752 | tf_op jit(solution)/shard_map/ppermute | solution.py:20
  388.0 8.9 %maximum_maximum_fusion.1 = (f32[5,128,10,256]{1,2,3,0:T(8,128)}, f32[5,128,10,256]{1,2,3,0:T(8,128)}) fusion(f32[1,128,8,256]{1,2,3,0:T(8,128)S(1)} %bitcast.147, f32[3,128,8,256]{1,2,3,0:T(8,128)S(1)} %copy.72, f32[1,128,8,256]{1,2,3,0:T(8,128)S(1)} %bitcast.142, f32[5,128,2,256]{1,2,3,0:T(2,128)} %collective-permute-done.2, ...), kind=kLoop, calls=%fused_computation.2 | loop fusion | flops 9830400 | bytes 20971520 | tf_op jit(solution)/shard_map/concatenate | solution.py:16
  396.9 0.5 broadcast.28
  397.5 16.8 %reduce = f32[8,163840]{1,0:T(8,128)} reduce(f32[8,1,163840]{2,1,0:T(1,128)} %all-to-all-done.1, f32[]{:T(128)} %broadcast.28), dimensions={1}, to_apply=%all_to_all.56.reduce_sub_computation | reduce | bytes 10485764 | tf_op jit(solution)/shard_map/all_to_all | solution.py:76
  414.3 16.3 %reshape.22 = f32[1024,5,8,32]{3,2,1,0:T(8,128)} reshape(f32[8,163840]{1,0:T(8,128)} %reduce) | data formatting | bytes 10485760
  430.6 14.0 %copy.109 = f32[5,128,8,8,32]{1,2,4,3,0:T(8,128)} copy(f32[5,128,8,8,32]{4,2,0,1,3:T(8,128)} %bitcast.139) | data formatting | bytes 10485760 | tf_op jit(solution)/shard_map/all_to_all | solution.py:76
  444.6 0.0 all-to-all-done.3
  444.6 5.6 %copy.95 = f32[5,128,8,16,16]{1,4,3,2,0:T(8,128)} copy(f32[5,128,8,16,16]{1,4,0,2,3:T(8,128)} %bitcast.39) | data formatting | bytes 10485760 | tf_op jit(solution)/shard_map/all_to_all | solution.py:83
  450.2 37.2 %fusion.10 = f32[5,128,8,256]{1,2,3,0:T(8,128)} fusion(f32[5,128,8,256]{1,2,3,0:T(8,128)} %bitcast.149, f32[5,128,8,2]{1,2,3,0:T(8,128)S(1)} %reshape.18, f32[5,128,8,256]{1,2,3,0:T(8,128)} %copy-done.7, f32[5,128,8,2]{1,2,3,0:T(8,128)S(1)} %reshape.17, f32[5,128,10,256]{1,2,3,0:T(8,128)} %get-tuple-element.27, f32[5,128,10,256]{1,2,3,0:T(8,128)} %get-tuple-element.26, ...), kind=kLoop, calls=%fused_computation.18 | loop fusion | flops 41943040 | bytes 68239872 | tf_op jit(solution)/shard_map/add | solution.py:88
  487.5 3.2 slice_bitcast_fusion
  490.6 2.4 copy.102
  493.0 2.6 copy.103
  495.6 2.6 copy.101
  (17 shorter events, 0.0 us)
Async XLA Ops:
  0.6 210.1 %copy-start = (f32[128,128]{1,0:T(8,128)S(1)}, f32[128,128]{1,0:T(8,128)}, u32[]{:S(2)}) copy-start(f32[128,128]{1,0:T(8,128)} %param.10) | copy-start | bytes 196612
  8.6 1.8 copy-start.2
  8.6 1.8 copy-start.5
  11.9 2.3 copy-start.7
  14.2 2.3 copy-start.8
  19.2 81.6 %all-to-all-start = ((f32[5,128,8,256]{1,2,0,3:T(8,128)}), f32[5,128,8,256]{1,2,0,3:T(8,128)}, u32[]{:S(2)}, u32[]{:S(2)}) async-start(f32[5,128,8,256]{1,2,0,3:T(8,128)} %copy.81), calls=%async_computation | async-start | bytes 10485760 | tf_op jit(solution)/shard_map/all_to_all | solution.py:73
  100.8 89.3 %all-to-all-start.2 = ((f32[5,128,8,256]{1,2,0,3:T(8,128)}), f32[5,128,8,256]{1,2,0,3:T(8,128)}, u32[]{:S(2)}, u32[]{:S(2)}) async-start(f32[5,128,8,256]{1,2,0,3:T(8,128)} %copy.89), calls=%async_computation.2 | async-start | bytes 10485760 | tf_op jit(solution)/shard_map/all_to_all | solution.py:80
  190.1 94.4 %all-to-all-start.1 = ((f32[8,1,163840]{2,1,0:T(1,128)}), f32[8,1,163840]{2,1,0:T(1,128)}, u32[]{:S(2)}, u32[]{:S(2)}) async-start(f32[8,1,163840]{2,1,0:T(1,128)} %reshape.21), calls=%async_computation.1 | async-start | bytes 10485760 | tf_op jit(solution)/shard_map/all_to_all | solution.py:76
  284.4 160.1 %all-to-all-start.3 = ((f32[5,128,128,16]{1,3,0,2:T(8,128)}), f32[5,128,128,16]{1,3,0,2:T(8,128)}, u32[]{:S(2)}, u32[]{:S(2)}) async-start(f32[5,128,128,16]{1,3,0,2:T(8,128)} %copy.93), calls=%async_computation.3 | async-start | bytes 10485760 | tf_op jit(solution)/shard_map/all_to_all | solution.py:83
  296.8 66.9 %collective-permute-start.2 = (f32[5,128,2,256]{1,2,3,0:T(2,128)}, f32[5,128,2,256]{1,2,3,0:T(2,128)}, u32[]{:S(2)}, u32[]{:S(2)}) collective-permute-start(f32[5,128,2,256]{1,2,3,0:T(2,128)} %get-tuple-element.28), channel_id=1, source_target_pairs={{0,1},{1,2},{2,3},{3,4},{4,5},{5,6},{6,7},{7,8},{8,9},{9,10},{10,1... | collective-permute-start | bytes 3932168 | tf_op jit(solution)/shard_map/ppermute | solution.py:18
  297.9 90.1 %collective-permute-start.3 = (f32[5,128,2,256]{1,2,3,0:T(2,128)}, f32[5,128,2,256]{1,2,3,0:T(2,128)}, u32[]{:S(2)}, u32[]{:S(2)}) collective-permute-start(f32[5,128,2,256]{1,2,3,0:T(2,128)} %get-tuple-element.29), channel_id=1, source_target_pairs={{1,0},{2,1},{3,2},{4,3},{5,4},{6,5},{7,6},{8,7},{9,8},{10,9},{11,1... | collective-permute-start | bytes 3932168 | tf_op jit(solution)/shard_map/ppermute | solution.py:20
  306.8 16.1 %collective-permute-start.1 = (f32[5,2,8,256]{3,2,1,0:T(8,128)S(1)}, f32[5,2,8,256]{3,2,1,0:T(8,128)S(1)}, u32[]{:S(2)}, u32[]{:S(2)}) collective-permute-start(f32[5,2,8,256]{3,2,1,0:T(8,128)S(1)} %copy.99), channel_id=1, source_target_pairs={{16,0},{32,16},{48,32},{64,48},{80,64},{96,80},{112,96},{17,1},{33... | collective-permute-start | bytes 245768 | tf_op jit(solution)/shard_map/ppermute | solution.py:20
  312.1 7.0 %collective-permute-start = (f32[5,2,8,256]{3,2,1,0:T(8,128)S(1)}, f32[5,2,8,256]{3,2,1,0:T(8,128)}, u32[]{:S(2)}, u32[]{:S(2)}) collective-permute-start(f32[5,2,8,256]{3,2,1,0:T(8,128)S(1)} %copy.97), channel_id=1, source_target_pairs={{0,16},{16,32},{32,48},{48,64},{64,80},{80,96},{96,112},{1,17},{17... | collective-permute-start | bytes 245768 | tf_op jit(solution)/shard_map/ppermute | solution.py:18
  326.1 61.9 %copy-start.3 = (f32[128,8,256]{0,1,2:T(8,128)S(1)}, f32[128,8,256]{0,1,2:T(8,128)}, u32[]{:S(2)}) copy-start(f32[128,8,256]{0,1,2:T(8,128)} %copy.70) | copy-start | bytes 3145732
  326.1 61.9 %copy-start.6 = (f32[128,8,256]{0,1,2:T(8,128)S(1)}, f32[128,8,256]{0,1,2:T(8,128)}, u32[]{:S(2)}) copy-start(f32[128,8,256]{0,1,2:T(8,128)} %copy.71) | copy-start | bytes 3145732
  444.6 5.7 %copy-start.4 = (f32[128,8,256]{0,1,2:T(8,128)S(1)}, f32[128,8,256]{0,1,2:T(8,128)}, u32[]{:S(2)}) copy-start(f32[128,8,256]{0,1,2:T(8,128)} %copy.70) | copy-start | bytes 3145732
  487.5 3.2 slice-start
  490.6 7.7 %copy-start.1 = (f32[128,128]{1,0:T(8,128)S(1)}, f32[128,128]{1,0:T(8,128)}, u32[]{:S(2)}) copy-start(f32[128,128]{1,0:T(8,128)} %param.10) | copy-start | bytes 196612
where the time goes:
time: 506 us; the launch traced here: 499 us
  waiting for transfers between devices  191 us (38%)
  local copies, waits for them, and re-layouts  143 us (28%)
  other arithmetic  82.7 us (16%)
  starting transfers between devices  47.6 us (9%)
  matrix products  33.4 us (7%)
    all_to_all x1, waiting for transfers between devices, local(): lax.all_to_all(upward, 'gy', split_axis=3, concat_axis=1, tiled=True)  71.1 us
    all_to_all x1, waiting for transfers between devices, local(): lax.all_to_all(derivative, 'gy', split_axis=1, concat_axis=3, tiled=True)  56.2 us
    unnamed x27, local copies, waits for them, and re-layouts  51.3 us
    add x1, other arithmetic, local(): advanced = conserved + time_step * tendency  37.2 us
    ppermute x2, waiting for transfers between devices, with_halo(): lax.ppermute(head, axis, [((i + 1) % count, i) for i in range(ends)])  24.3 us
    concatenate x2, other arithmetic, with_halo(): jnp.concatenate([lax.ppermute(tail, axis, [(i, (i + 1) % count) for i in...  23.5 us
    ppermute x2, waiting for transfers between devices, with_halo(): lax.ppermute(tail, axis, [(i, (i + 1) % count) for i in range(ends)])  23 us
    dot_general x1, matrix products, local(): jnp.einsum('ij,fjzx->fizx', wall_operator, lax.all_to_all(upward, 'gy', s...  22 us
  transfers between devices with their start and end apart: 8, of which 5 were waited for; matrix products, arithmetic and copies ran while one was open for 36% of the time, Pallas kernels for 0%

commit v1 on v0

--- a/solution.py
+++ b/solution.py
@@ -73,7 +73,10 @@
         lax.all_to_all(upward, "gy", split_axis=3, concat_axis=1, tiled=True),
         precision=lax.Precision.HIGHEST,
     )
-    deriv_y = lax.all_to_all(derivative, "gy", split_axis=1, concat_axis=3, tiled=True)
+    deriv_y = jnp.concatenate(
+        lax.all_to_all(jnp.stack(jnp.split(derivative, lax.axis_size("gy"), axis=1)), "gy", 0, 0),
+        axis=3,
+    )
     derivative = jnp.einsum(
         "ij,fyjx->fyix",
         span_operator,

time: 506 us -> 459 us (0.907)
  local copies, waits for them, and re-layouts: 143 us -> 98 us
  waiting for transfers between devices: 191 us -> 219 us
  other arithmetic: 82.7 us -> 67.3 us
  starting transfers between devices: 47.6 us -> 34.6 us
    all_to_all x1, waiting for transfers between devices: 15.9 us -> 43.4 us  [local(): lax.all_to_all(sideways, 'gz', split_axis=3, concat_axis=2, tiled=True)]
    unnamed x27 -> x32, local copies, waits for them, and re-layouts: 51.3 us -> 27.2 us
    all_to_all x1 -> x0, other arithmetic: 16.8 us -> none  [local(): lax.all_to_all(derivative, 'gy', split_axis=1, concat_axis=3, tiled=True)]
    all_to_all x2 -> x0, local copies, waits for them, and re-layouts: 14.5 us -> none  [local(): lax.all_to_all(derivative, 'gy', split_axis=1, concat_axis=3, tiled=True)]
    transpose x1 -> x0, local copies, waits for them, and re-layouts: 13.3 us -> none  [local(): jnp.einsum('ij,fjzx->fizx', wall_operator, lax.all_to_all(upward, 'gy', s...]
    all_to_all x1, starting transfers between devices: 16.9 us -> 4.77 us  [local(): lax.all_to_all(jnp.stack(jnp.split(derivative, lax.axis_size('gy'), axis=...]
    reshape x0 -> x1, local copies, waits for them, and re-layouts: none -> 5.67 us  [local(): jnp.concatenate(lax.all_to_all(jnp.stack(jnp.split(derivative, lax.axis_s...]
  transfers between devices with their start and end apart: 8 -> 8, of which waited for: 5 -> 5; matrix products, arithmetic and copies ran while one was open for 36% -> 26% of each run, Pallas kernels for 0% -> 0%
where the time goes in v1:
time: 459 us; the launch traced here: 452 us
  waiting for transfers between devices  219 us (48%)
  local copies, waits for them, and re-layouts  98 us (21%)
  other arithmetic  67.3 us (15%)
  starting transfers between devices  34.6 us (8%)
  matrix products  32.5 us (7%)
    all_to_all x1, waiting for transfers between devices, local(): lax.all_to_all(upward, 'gy', split_axis=3, concat_axis=1, tiled=True)  71.1 us
    all_to_all x1, waiting for transfers between devices, local(): lax.all_to_all(jnp.stack(jnp.split(derivative, lax.axis_size('gy'), axis=...  57.3 us
    all_to_all x1, waiting for transfers between devices, local(): lax.all_to_all(sideways, 'gz', split_axis=3, concat_axis=2, tiled=True)  43.4 us
    add x1, other arithmetic, local(): advanced = conserved + time_step * tendency  38.6 us
    unnamed x32, local copies, waits for them, and re-layouts  27.2 us
    ppermute x2, waiting for transfers between devices, with_halo(): lax.ppermute(head, axis, [((i + 1) % count, i) for i in range(ends)])  24.3 us
    concatenate x2, other arithmetic, with_halo(): jnp.concatenate([lax.ppermute(tail, axis, [(i, (i + 1) % count) for i in...  23.5 us
    ppermute x2, waiting for transfers between devices, with_halo(): lax.ppermute(tail, axis, [(i, (i + 1) % count) for i in range(ends)])  22.6 us
  transfers between devices with their start and end apart: 8, of which 5 were waited for; matrix products, arithmetic and copies ran while one was open for 26% of the time, Pallas kernels for 0%

profile of v1, /device:TPU:87, one launch (start us, length us, event | category | flops | bytes accessed | tf_op | source)
XLA Modules:
  0.0 452.3 jit_solution(12849946512065513995)
XLA Ops:
  0.6 0.0 copy-start
  0.6 2.7 copy.37
  3.3 2.6 copy.38
  5.9 2.6 copy.39
  8.5 0.0 copy-start.2
  8.5 0.0 copy-start.5
  8.5 0.1 slice_dynamic-update-slice_fusion
  8.7 1.5 bitcast_dynamic-update-slice_fusion.7
  10.2 0.2 copy-done.5
  10.4 0.7 bitcast_dynamic-update-slice_fusion.3
  11.0 0.3 bitcast_dynamic-update-slice_fusion.2
  11.3 0.4 bitcast_dynamic-update-slice_fusion.11
  11.7 0.1 bitcast_dynamic-update-slice_fusion.10
  11.8 0.1 bitcast_dynamic-update-slice_fusion.9
  11.9 0.3 bitcast_dynamic-update-slice_fusion.4
  12.2 2.4 copy-done.7
  14.6 2.4 copy-done.8
  17.0 2.6 copy.48
  19.6 5.3 %all-to-all-start = ((f32[5,128,8,256]{1,2,0,3:T(8,128)}), f32[5,128,8,256]{1,2,0,3:T(8,128)}, u32[]{:S(2)}, u32[]{:S(2)}) async-start(f32[5,128,8,256]{1,2,0,3:T(8,128)} %copy.48), calls=%async_computation | async-start | bytes 10485760 | tf_op jit(solution)/shard_map/all_to_all | solution.py:73
  24.8 5.2 %copy.54 = f32[5,128,8,256]{1,2,0,3:T(8,128)} copy(f32[5,128,8,256]{1,2,3,0:T(8,128)} %copy-done.8) | data formatting | bytes 10485760 | tf_op jit(solution)/shard_map/stack | solution.py:42
  30.0 71.1 %all-to-all-done = f32[5,128,8,256]{1,2,0,3:T(8,128)} async-done(((f32[5,128,8,256]{1,2,0,3:T(8,128)}), f32[5,128,8,256]{1,2,0,3:T(8,128)}, u32[]{:S(2)}, u32[]{:S(2)}) %all-to-all-start) | async-done | bytes 5242912 | tf_op jit(solution)/shard_map/all_to_all | solution.py:73
  101.1 8.7 %all-to-all-start.2 = ((f32[5,128,8,256]{1,2,0,3:T(8,128)}), f32[5,128,8,256]{1,2,0,3:T(8,128)}, u32[]{:S(2)}, u32[]{:S(2)}) async-start(f32[5,128,8,256]{1,2,0,3:T(8,128)} %copy.54), calls=%async_computation.2 | async-start | bytes 10485760 | tf_op jit(solution)/shard_map/all_to_all | solution.py:83
  109.8 7.8 %copy.50 = f32[5,8,128,8,32]{2,1,4,3,0:T(8,128)} copy(f32[5,8,128,8,32]{2,3,0,4,1:T(8,128)} %bitcast.17) | data formatting | bytes 10485760 | tf_op jit(solution)/shard_map/all_to_all | solution.py:73
  117.6 6.7 %all_to_all.45 = f32[5,1024,8,32]{1,3,2,0:T(8,128)} reshape(f32[5,8,128,8,32]{2,1,4,3,0:T(8,128)} %copy.50) | data formatting | bytes 10485760 | tf_op jit(solution)/shard_map/all_to_all | solution.py:73
  124.4 21.1 %fusion.25 = f32[5,1024,8,32]{1,3,2,0:T(8,128)S(1)} fusion(f32[5,1024,8,32]{1,3,2,0:T(8,128)} %all_to_all.45, f32[1024,1024]{1,0:T(8,128)} %param.9), kind=kOutput, calls=%fused_computation.42 | convolution fusion | flops 16106127360 | bytes 14680064 | tf_op jit(solution)/shard_map/ij,fjzx->fizx/dot_general | solution.py:70
  145.5 0.9 fusion.47
  146.5 0.9 fusion.46
  147.4 0.9 fusion.45
  148.3 1.0 fusion.44
  149.3 0.9 fusion.43
  150.3 0.9 fusion.42
  151.2 0.9 fusion.41
  152.1 0.9 fusion.40
  153.1 43.4 %all-to-all-done.2 = f32[5,128,8,256]{1,2,0,3:T(8,128)} async-done(((f32[5,128,8,256]{1,2,0,3:T(8,128)}), f32[5,128,8,256]{1,2,0,3:T(8,128)}, u32[]{:S(2)}, u32[]{:S(2)}) %all-to-all-start.2) | async-done | bytes 5242912 | tf_op jit(solution)/shard_map/all_to_all | solution.py:83
  196.4 4.8 %all-to-all-start.1 = ((f32[8,5,128,8,32]{2,4,3,1,0:T(8,128)}), f32[8,5,128,8,32]{2,4,3,1,0:T(8,128)}, u32[]{:S(2)}, u32[]{:S(2)}) async-start(f32[8,5,128,8,32]{2,4,3,1,0:T(8,128)} %fusion.40), calls=%async_computation.1 | async-start | bytes 10485760 | tf_op jit(solution)/shard_map/all_to_all | solution.py:77
  201.2 3.7 copy.56
  204.9 11.4 %fusion.28 = f32[5,128,128,16]{2,1,3,0:T(8,128)} fusion(f32[5,128,128,16]{1,3,2,0:T(8,128)S(1)} %bitcast.174, f32[128,128]{1,0:T(8,128)S(1)} %copy-done), kind=kOutput, calls=%fused_computation.43 | convolution fusion | flops 2013265920 | bytes 10551296 | tf_op jit(solution)/shard_map/ij,fyjx->fyix/dot_general | solution.py:80
  216.3 6.1 %copy.58 = f32[5,128,128,16]{1,3,0,2:T(8,128)} copy(f32[5,128,128,16]{2,1,3,0:T(8,128)} %fusion.28) | data formatting | bytes 10485760 | tf_op jit(solution)/shard_map/ij,fyjx->fyix/transpose | solution.py:80
  222.4 57.3 %all-to-all-done.1 = f32[8,5,128,8,32]{2,4,3,1,0:T(8,128)} async-done(((f32[8,5,128,8,32]{2,4,3,1,0:T(8,128)}), f32[8,5,128,8,32]{2,4,3,1,0:T(8,128)}, u32[]{:S(2)}, u32[]{:S(2)}) %all-to-all-start.1) | async-done | bytes 5242912 | tf_op jit(solution)/shard_map/all_to_all | solution.py:77
  279.8 7.3 %all-to-all-start.3 = ((f32[5,128,128,16]{1,3,0,2:T(8,128)}), f32[5,128,128,16]{1,3,0,2:T(8,128)}, u32[]{:S(2)}, u32[]{:S(2)}) async-start(f32[5,128,128,16]{1,3,0,2:T(8,128)} %copy.58), calls=%async_computation.3 | async-start | bytes 10485760 | tf_op jit(solution)/shard_map/all_to_all | solution.py:86
  287.1 1.9 pad_maximum_fusion.4
  289.0 2.3 fusion.51
  291.3 1.2 collective-permute-start.2
  292.4 0.0 collective-permute-start.3
  292.4 5.7 %fusion.50 = (f32[5,2,8,256]{1,2,3,0:T(8,128)}, f32[5,2,8,256]{1,2,3,0:T(8,128)}) fusion(f32[5,128,8,256]{1,2,3,0:T(8,128)S(1)} %pad_maximum_fusion.4), kind=kLoop, calls=%fused_computation.104 | loop fusion | bytes 327680 | tf_op jit(solution)/shard_map/slice | solution.py:15
  298.1 3.3 copy.64
  301.4 1.9 collective-permute-start.1
  303.4 3.5 copy.62
  306.9 5.5 %collective-permute-start = (f32[5,2,8,256]{3,2,1,0:T(8,128)S(1)}, f32[5,2,8,256]{3,2,1,0:T(8,128)}, u32[]{:S(2)}, u32[]{:S(2)}) collective-permute-start(f32[5,2,8,256]{3,2,1,0:T(8,128)S(1)} %copy.62), channel_id=1, source_target_pairs={{0,16},{16,32},{32,48},{48,64},{64,80},{80,96},{96,112},{1,17},{17... | collective-permute-start | bytes 245768 | tf_op jit(solution)/shard_map/ppermute | solution.py:18
  312.4 0.8 slice_bitcast_fusion.11
  313.1 0.8 dynamic_slice.3
  313.9 3.9 copy.63
  317.8 3.2 copy.65
  321.0 14.6 %maximum_maximum_fusion = (f32[5,130,8,256]{1,2,3,0:T(8,128)}, f32[5,130,8,256]{1,2,3,0:T(8,128)}) fusion(f32[1,128,8,256]{1,2,3,0:T(8,128)} %bitcast.169, f32[3,128,8,256]{1,2,3,0:T(8,128)S(1)} %copy.39, f32[1,128,8,256]{1,2,3,0:T(8,128)} %bitcast.165, f32[5,2,8,256]{1,2,3,0:T(8,128)} %copy.63, f32[5,2,8,256]{1,2,3,0:T(8,128)} %copy.65), kind=kLoop, calls=%fused_computation | loop fusion | flops 7987200 | bytes 16056320 | tf_op jit(solution)/shard_map/concatenate | solution.py:16
  335.6 22.6 %collective-permute-done.2 = f32[5,128,2,256]{1,2,3,0:T(2,128)} collective-permute-done((f32[5,128,2,256]{1,2,3,0:T(2,128)}, f32[5,128,2,256]{1,2,3,0:T(2,128)}, u32[]{:S(2)}, u32[]{:S(2)}) %collective-permute-start.2) | collective-permute-done | bytes 1310752 | tf_op jit(solution)/shard_map/ppermute | solution.py:18
  358.2 24.3 %collective-permute-done.3 = f32[5,128,2,256]{1,2,3,0:T(2,128)} collective-permute-done((f32[5,128,2,256]{1,2,3,0:T(2,128)}, f32[5,128,2,256]{1,2,3,0:T(2,128)}, u32[]{:S(2)}, u32[]{:S(2)}) %collective-permute-start.3) | collective-permute-done | bytes 1310752 | tf_op jit(solution)/shard_map/ppermute | solution.py:20
  382.5 8.9 %maximum_maximum_fusion.1 = (f32[5,128,10,256]{1,2,3,0:T(8,128)}, f32[5,128,10,256]{1,2,3,0:T(8,128)}) fusion(f32[1,128,8,256]{1,2,3,0:T(8,128)S(1)} %bitcast.171, f32[3,128,8,256]{1,2,3,0:T(8,128)S(1)} %copy.39, f32[1,128,8,256]{1,2,3,0:T(8,128)S(1)} %bitcast.166, f32[5,128,2,256]{1,2,3,0:T(2,128)} %collective-permute-done.2, ...), kind=kLoop, calls=%fused_computation.2 | loop fusion | flops 9830400 | bytes 20971520 | tf_op jit(solution)/shard_map/concatenate | solution.py:16
  391.4 5.7 %copy.51 = f32[5,128,8,8,32]{1,4,3,2,0:T(8,128)} copy(f32[5,128,8,8,32]{1,4,2,0,3:T(8,128)} %bitcast.29) | data formatting | bytes 10485760 | tf_op jit(solution)/shard_map/reshape | solution.py:76
  397.1 5.6 %copy.60 = f32[5,128,8,16,16]{1,4,3,2,0:T(8,128)} copy(f32[5,128,8,16,16]{1,4,0,2,3:T(8,128)} %bitcast.44) | data formatting | bytes 10485760 | tf_op jit(solution)/shard_map/all_to_all | solution.py:86
  402.7 38.6 %fusion.10 = f32[5,128,8,256]{1,2,3,0:T(8,128)} fusion(f32[5,128,8,2]{1,2,3,0:T(8,128)S(1)} %reshape.24, f32[5,128,8,256]{1,2,3,0:T(8,128)} %copy-done.7, f32[5,128,8,2]{1,2,3,0:T(8,128)S(1)} %reshape.23, f32[5,128,10,256]{1,2,3,0:T(8,128)} %get-tuple-element.24, f32[5,128,10,256]{1,2,3,0:T(8,128)} %get-tuple-element.23, ...), kind=kLoop, calls=%fused_computation.18 | loop fusion | flops 41943040 | bytes 68239872 | tf_op jit(solution)/shard_map/add | solution.py:91
  441.2 3.2 slice_bitcast_fusion
  444.4 2.4 copy.67
  446.8 2.6 copy.68
  449.4 2.6 copy.66
  (19 shorter events, 0.0 us)
Async XLA Ops:
  0.6 204.3 %copy-start = (f32[128,128]{1,0:T(8,128)S(1)}, f32[128,128]{1,0:T(8,128)}, u32[]{:S(2)}) copy-start(f32[128,128]{1,0:T(8,128)} %param.10) | copy-start | bytes 196612
  8.5 1.7 copy-start.2
  8.5 1.8 copy-start.5
  12.2 2.4 copy-start.7
  14.6 2.4 copy-start.8
  19.6 81.6 %all-to-all-start = ((f32[5,128,8,256]{1,2,0,3:T(8,128)}), f32[5,128,8,256]{1,2,0,3:T(8,128)}, u32[]{:S(2)}, u32[]{:S(2)}) async-start(f32[5,128,8,256]{1,2,0,3:T(8,128)} %copy.48), calls=%async_computation | async-start | bytes 10485760 | tf_op jit(solution)/shard_map/all_to_all | solution.py:73
  101.1 95.3 %all-to-all-start.2 = ((f32[5,128,8,256]{1,2,0,3:T(8,128)}), f32[5,128,8,256]{1,2,0,3:T(8,128)}, u32[]{:S(2)}, u32[]{:S(2)}) async-start(f32[5,128,8,256]{1,2,0,3:T(8,128)} %copy.54), calls=%async_computation.2 | async-start | bytes 10485760 | tf_op jit(solution)/shard_map/all_to_all | solution.py:83
  196.4 83.3 %all-to-all-start.1 = ((f32[8,5,128,8,32]{2,4,3,1,0:T(8,128)}), f32[8,5,128,8,32]{2,4,3,1,0:T(8,128)}, u32[]{:S(2)}, u32[]{:S(2)}) async-start(f32[8,5,128,8,32]{2,4,3,1,0:T(8,128)} %fusion.40), calls=%async_computation.1 | async-start | bytes 10485760 | tf_op jit(solution)/shard_map/all_to_all | solution.py:77
  279.8 117.3 %all-to-all-start.3 = ((f32[5,128,128,16]{1,3,0,2:T(8,128)}), f32[5,128,128,16]{1,3,0,2:T(8,128)}, u32[]{:S(2)}, u32[]{:S(2)}) async-start(f32[5,128,128,16]{1,3,0,2:T(8,128)} %copy.58), calls=%async_computation.3 | async-start | bytes 10485760 | tf_op jit(solution)/shard_map/all_to_all | solution.py:86
  291.3 66.9 %collective-permute-start.2 = (f32[5,128,2,256]{1,2,3,0:T(2,128)}, f32[5,128,2,256]{1,2,3,0:T(2,128)}, u32[]{:S(2)}, u32[]{:S(2)}) collective-permute-start(f32[5,128,2,256]{1,2,3,0:T(2,128)} %get-tuple-element.25), channel_id=1, source_target_pairs={{0,1},{1,2},{2,3},{3,4},{4,5},{5,6},{6,7},{7,8},{8,9},{9,10},{10,1... | collective-permute-start | bytes 3932168 | tf_op jit(solution)/shard_map/ppermute | solution.py:18
  292.4 90.1 %collective-permute-start.3 = (f32[5,128,2,256]{1,2,3,0:T(2,128)}, f32[5,128,2,256]{1,2,3,0:T(2,128)}, u32[]{:S(2)}, u32[]{:S(2)}) collective-permute-start(f32[5,128,2,256]{1,2,3,0:T(2,128)} %get-tuple-element.26), channel_id=1, source_target_pairs={{1,0},{2,1},{3,2},{4,3},{5,4},{6,5},{7,6},{8,7},{9,8},{10,9},{11,1... | collective-permute-start | bytes 3932168 | tf_op jit(solution)/shard_map/ppermute | solution.py:20
  301.4 16.4 %collective-permute-start.1 = (f32[5,2,8,256]{3,2,1,0:T(8,128)S(1)}, f32[5,2,8,256]{3,2,1,0:T(8,128)S(1)}, u32[]{:S(2)}, u32[]{:S(2)}) collective-permute-start(f32[5,2,8,256]{3,2,1,0:T(8,128)S(1)} %copy.64), channel_id=1, source_target_pairs={{16,0},{32,16},{48,32},{64,48},{80,64},{96,80},{112,96},{17,1},{33... | collective-permute-start | bytes 245768 | tf_op jit(solution)/shard_map/ppermute | solution.py:20
  306.9 7.0 %collective-permute-start = (f32[5,2,8,256]{3,2,1,0:T(8,128)S(1)}, f32[5,2,8,256]{3,2,1,0:T(8,128)}, u32[]{:S(2)}, u32[]{:S(2)}) collective-permute-start(f32[5,2,8,256]{3,2,1,0:T(8,128)S(1)} %copy.62), channel_id=1, source_target_pairs={{0,16},{16,32},{32,48},{48,64},{64,80},{80,96},{96,112},{1,17},{17... | collective-permute-start | bytes 245768 | tf_op jit(solution)/shard_map/ppermute | solution.py:18
  321.0 61.6 %copy-start.3 = (f32[128,8,256]{0,1,2:T(8,128)S(1)}, f32[128,8,256]{0,1,2:T(8,128)}, u32[]{:S(2)}) copy-start(f32[128,8,256]{0,1,2:T(8,128)} %copy.37) | copy-start | bytes 3145732
  321.0 61.6 %copy-start.6 = (f32[128,8,256]{0,1,2:T(8,128)S(1)}, f32[128,8,256]{0,1,2:T(8,128)}, u32[]{:S(2)}) copy-start(f32[128,8,256]{0,1,2:T(8,128)} %copy.38) | copy-start | bytes 3145732
  397.1 5.6 %copy-start.4 = (f32[128,8,256]{0,1,2:T(8,128)S(1)}, f32[128,8,256]{0,1,2:T(8,128)}, u32[]{:S(2)}) copy-start(f32[128,8,256]{0,1,2:T(8,128)} %copy.37) | copy-start | bytes 3145732
  441.2 3.2 slice-start
  444.4 7.7 %copy-start.1 = (f32[128,128]{1,0:T(8,128)S(1)}, f32[128,128]{1,0:T(8,128)}, u32[]{:S(2)}) copy-start(f32[128,128]{1,0:T(8,128)} %param.10) | copy-start | bytes 196612
